TPU v7x, 256 devices: a whole 4x4x8 slice. The times are simulated.
256 devices in a mesh: members: 16 (over z_hi, y, core), lat: 4 (over x), blk: 4 (over z_lo).
Axes of the slice: x: 4, y: 4, z: 8 (z_hi: 2, z_lo: 4; z = z_hi * 4 + z_lo), core: 2. Of those that a mesh axis runs over, the one named last changes fastest.
Arguments:
- starting_states: float32 [512, 256, 768], P(('members', 'blk'), 'lat'), may hold values from -6 to 6
- courant_x: float32 [256, 768], P('lat'), may hold values from -0.3 to 0.3
- courant_y: float32 [256, 768], P('lat'), may hold values from -0.3 to 0.3
- diffusion: float32 [256, 768], P('lat'), may hold values from 0.05 to 0.2
- obs_index: int32 [4, 64, 128], P('lat', ('members', 'blk')), may hold values from 0 to 767
- obs_value: float32 [4, 64, 128], P('lat', ('members', 'blk')), may hold values from -6 to 6
- loc_weight: float32 [4, 64, 3, 128], P('lat', ('members', 'blk')), may hold values from 0.1 to 1
Outputs:
- analysis: float32 [512, 256, 768], P(('members', 'blk'), 'lat')
Inputs may be any that keep to these rules, and one draw needn't show every extreme that they name: `obs_index`: positions among the 768 cells of the block, counted row by row; repeats may occur.
All inputs are finite; a program needn't handle non-finite values.
Results may differ from a plain program's by a relative error of at most 0.0003.
Values sent between devices are 32-bit elements; how exact they have to be, the bound alone decides.
A program may use at most 64 MiB of HBM per device.

v0:
```python
import functools

import jax
import jax.numpy as jnp
from jax import lax
from jax.experimental import pallas as pl
from jax.experimental.pallas import tpu as pltpu
from jax.sharding import PartitionSpec as P

FSTEPS = 8
NS_ITERS = 4
ROWS = 16
AHEAD = 16
MESH = pl.DeviceIdType.MESH
VMEM = pl.BlockSpec(memory_space=pltpu.VMEM)
F32 = jnp.float32
BF16 = jnp.bfloat16


def split(x):
    high = x.astype(BF16)
    return high, (x - high.astype(F32)).astype(BF16)


def dot3(a, b, contract=((1,), (0,))):
    def one(p, q):
        return lax.dot_general(p, q, (contract, ((), ())), preferred_element_type=F32)

    return one(a[0], b[0]) + (one(a[0], b[1]) + one(a[1], b[0]))


def whole_kernel(
    state_ref, cx_ref, cy_ref, d_ref, index_ref, terms_ref, out_ref,
    levels, dense, coef, cells, obs, terms, block, seen, stack, result,
    gram, left_hi, left_lo, right_hi, right_lo, inv_hi, inv_lo, wide_hi, wide_lo, anom_hi, anom_lo,
    load_sem, coef_sem, send_sem, edge_send, edge_recv, cell_sem, term_sem, obs_sem, field_sem, low_sem, high_sem, back_sem,
):
    per, count, lon = state_ref.shape
    members = count * per
    tall = count + 2 * FSTEPS
    lo = lax.axis_index("members")
    bl = lax.axis_index("blk")
    lat = lax.axis_index("lat")
    n_lat = lax.axis_size("lat")
    n_blk = lax.axis_size("blk")
    me = lo * n_blk + bl
    my_z, my_y, my_core = (lo // 8) * 4 + bl, (lo // 2) % 4, lo % 2

    def set_at(z, y, core):
        return (((z // 4) * 4 + y) * 2 + core) * 4 + z % 4

    def block_at(z, y, core):
        return (z * 4 + y + (z % 2) * (3 - 2 * y)) * 2 + core

    def own_of(b):
        z, y = b // 8, (b // 2) % 4
        return set_at(z, y + (z % 2) * (3 - 2 * y), b % 2)

    def place(k):
        return {"members": k // n_blk, "blk": k % n_blk}

    def peer_of(t):
        dz, dcore, dy = t % 8, (t // 8) % 2, t // 16
        at = (my_z + dz) % 8, (my_y + dy) % 4, (my_core + dcore) % 2
        return set_at(*at), block_at(*at)

    mine = block_at(my_z, my_y, my_core)
    my_rows = pl.ds(pl.multiple_of(me * per, per), per)
    inner = pl.ds(FSTEPS, count)

    for m in range(per):
        pltpu.make_async_copy(state_ref.at[m], levels.at[inner, m, :], load_sem).start()

    barrier = pltpu.get_barrier_semaphore()

    def greet(t, carry):
        k, _ = peer_of(t)
        pl.semaphore_signal(barrier, inc=1, device_id=place(k), device_id_type=MESH)
        return carry

    @pl.when(lat > 0)
    def _():
        pl.semaphore_signal(barrier, inc=1, device_id={"lat": lat - 1}, device_id_type=MESH)

    @pl.when(lat < n_lat - 1)
    def _():
        pl.semaphore_signal(barrier, inc=1, device_id={"lat": lat + 1}, device_id_type=MESH)

    lax.fori_loop(1, count, greet, 0)

    cx, cy, d = 0.5 * cx_ref[...], 0.5 * cy_ref[...], d_ref[...]
    for i, value in enumerate((1.0 - 4.0 * d, d - cx, d + cx, d - cy, d + cy)):
        dense[i] = value
        pltpu.make_async_copy(dense.at[i], coef.at[inner, i, :], coef_sem).start()
    cells[me] = index_ref[0]
    low_rows, high_rows = pl.ds(0, FSTEPS), pl.ds(FSTEPS + count, FSTEPS)

    @pl.when(lat == 0)
    def _():
        levels[low_rows] = jnp.zeros((FSTEPS, per, lon), F32)
        coef[low_rows] = jnp.zeros((FSTEPS, per, lon), F32)

    @pl.when(lat == n_lat - 1)
    def _():
        levels[high_rows] = jnp.zeros((FSTEPS, per, lon), F32)
        coef[high_rows] = jnp.zeros((FSTEPS, per, lon), F32)

    pltpu.make_async_copy(levels.at[inner], levels.at[inner], load_sem).wait()
    pltpu.make_async_copy(dense, dense, coef_sem).wait()
    pl.semaphore_wait(
        barrier, count - 1 + jnp.where(lat > 0, 1, 0) + jnp.where(lat < n_lat - 1, 1, 0)
    )

    def edges(up):
        source = pl.ds(count if up else FSTEPS, FSTEPS)
        target = low_rows if up else high_rows
        side = 0 if up else 1
        device = {"lat": lat + 1 if up else lat - 1}
        return [
            pltpu.make_async_remote_copy(
                levels.at[source], levels.at[target], edge_send.at[side, 0], edge_recv.at[side, 0],
                device_id=device, device_id_type=MESH,
            ),
            pltpu.make_async_remote_copy(
                coef.at[source], coef.at[target], edge_send.at[side, 1],
                edge_recv.at[side, 1], device_id=device, device_id_type=MESH,
            ),
        ]

    @pl.when(lat < n_lat - 1)
    def _():
        for copy in edges(True):
            copy.start()

    @pl.when(lat > 0)
    def _():
        for copy in edges(False):
            copy.start()

    def send_cells(t, carry):
        k, _ = peer_of(t)
        pltpu.make_async_remote_copy(
            index_ref.at[0], cells.at[me], send_sem.at[5], cell_sem,
            device_id=place(k), device_id_type=MESH,
        ).start()
        return carry

    lax.fori_loop(1, count, send_cells, 0)

    def send_terms():
        return pltpu.make_async_remote_copy(
            terms_ref, terms, send_sem.at[6], term_sem,
            device_id=place(own_of(me)), device_id_type=MESH,
        )

    @pl.when(mine == me)
    def _():
        terms[...] = terms_ref[...]

    @pl.when(mine != me)
    def _():
        send_terms().start()

    lane = lax.broadcasted_iota(jnp.int32, (per, 128), 1)
    parts = lon // 128

    def advance_row(step, r):
        now = (step - 1) * tall + r
        pieces = [levels[now, :, p * 128 : (p + 1) * 128] for p in range(parts)]
        right = [pltpu.roll(v, 1, 1) for v in pieces]
        left = [pltpu.roll(v, 127, 1) for v in pieces]
        for p in range(parts):
            here = slice(p * 128, (p + 1) * 128)
            west = jnp.where(lane == 0, right[p - 1], right[p])
            east = jnp.where(lane == 127, left[(p + 1) % parts], left[p])
            c = [jnp.broadcast_to(coef[r, pl.ds(i, 1), here], lane.shape) for i in range(5)]
            levels[now + tall, :, here] = (
                (c[0] * pieces[p] + c[1] * east)
                + (c[2] * west + c[3] * levels[now + 1, :, here])
                + c[4] * levels[now - 1, :, here]
            )

    def inner_step(step, carry):
        low, high = FSTEPS + step, FSTEPS + count - step

        def rows(i, inner_carry):
            start = jnp.minimum(low + ROWS * i, high - ROWS)
            for u in range(ROWS):
                advance_row(step, start + u)
            return inner_carry

        return lax.fori_loop(0, (high - low + ROWS - 1) // ROWS, rows, carry)

    lax.fori_loop(1, FSTEPS + 1, inner_step, 0)

    @pl.when(lat > 0)
    def _():
        for copy in edges(True):
            copy.wait_recv()
        for copy in edges(False):
            copy.wait_send()

    @pl.when(lat < n_lat - 1)
    def _():
        for copy in edges(False):
            copy.wait_recv()
        for copy in edges(True):
            copy.wait_send()

    def edge_step(step, carry):
        for u in range(FSTEPS):
            advance_row(step, step + u)
            advance_row(step, tall - step - FSTEPS + u)
        return carry

    lax.fori_loop(1, FSTEPS + 1, edge_step, 0)
    final = FSTEPS * tall + FSTEPS

    pltpu.make_async_copy(cells.at[: count - 1], cells.at[: count - 1], cell_sem).wait()

    def observe(i, carry):
        for u in range(8):
            k = i * 8 + u
            b = k
            index = jnp.broadcast_to(cells[k], lane.shape)
            where, group = jnp.bitwise_and(index, 127), jnp.right_shift(index, 7)
            found = jnp.zeros(lane.shape, F32)
            for p in range(parts):
                picked = jnp.take_along_axis(
                    levels[final + b, :, p * 128 : (p + 1) * 128], where, axis=1
                )
                found = jnp.where(group == p, picked, found)
            obs[b] = found
        return carry

    lax.fori_loop(0, count // 8, observe, 0)

    def send_obs(t, carry):
        k, b = peer_of(t)
        pltpu.make_async_remote_copy(
            obs.at[b], seen.at[my_rows, :], send_sem.at[0], obs_sem,
            device_id=place(k), device_id_type=MESH,
        ).start()
        return carry

    def send_field(t, carry):
        k, b = peer_of(t)
        pltpu.make_async_remote_copy(
            levels.at[final + b], block.at[my_rows, :], send_sem.at[1], field_sem,
            device_id=place(k), device_id_type=MESH,
        ).start()
        return carry

    lax.fori_loop(1, count, send_obs, 0)
    lax.fori_loop(1, AHEAD, send_field, 0)
    seen[my_rows, :] = obs[mine]
    block[my_rows, :] = levels[final + mine]

    @pl.when(mine != me)
    def _():
        send_terms().wait()

    others = (count - 1) * per
    pltpu.make_async_copy(seen.at[:others], seen.at[:others], obs_sem).wait()

    ybar = jnp.mean(seen[...], axis=0, keepdims=True)
    own = seen[...] - ybar
    stack[1, :members, :] = own
    stack[1, members:, :] = jnp.broadcast_to(terms[pl.ds(0, 1), :] - ybar, (8, own.shape[1]))

    def to_low():
        return pltpu.make_async_remote_copy(
            stack.at[1], stack.at[2], send_sem.at[2], high_sem,
            device_id=place(own_of(mine - 1)), device_id_type=MESH,
        )

    def to_high():
        return pltpu.make_async_remote_copy(
            stack.at[1], stack.at[0], send_sem.at[3], low_sem,
            device_id=place(own_of(mine + 1)), device_id_type=MESH,
        )

    @pl.when(mine > 0)
    def _():
        to_low().start()

    @pl.when(mine < count - 1)
    def _():
        to_high().start()

    lax.fori_loop(AHEAD, count, send_field, 0)

    @pl.when(mine == 0)
    def _():
        stack[0] = jnp.zeros(stack.shape[1:], F32)

    @pl.when(mine == count - 1)
    def _():
        stack[2] = jnp.zeros(stack.shape[1:], F32)

    @pl.when(mine > 0)
    def _():
        to_low().wait_send()
        to_high().wait_recv()

    @pl.when(mine < count - 1)
    def _():
        to_high().wait_send()
        to_low().wait_recv()

    obs = own.shape[1]
    pull = jnp.zeros((members, 1), F32)
    for part in range(3):
        held = stack[part, :members, :]
        weighted = held * terms[pl.ds(1 + part, 1), :]
        pull = pull + jnp.sum(weighted * stack[part, pl.ds(members, 1), :], axis=1, keepdims=True)
        here = slice(part * obs, (part + 1) * obs)
        wide_hi[:, here], wide_lo[:, here] = split(held)
        left_hi[:, here], left_lo[:, here] = split(weighted)

    rows = 128
    chunks = members // rows

    def eye(start):
        row = lax.broadcasted_iota(jnp.int32, (rows, members), 0) + start
        return (row == lax.broadcasted_iota(jnp.int32, (rows, members), 1)).astype(F32)

    def at(i):
        return pl.ds(pl.multiple_of(i * rows, rows), rows)

    width = 3 * obs

    def gram_rows(i, total):
        part = dot3(
            (left_hi[at(i), :width], left_lo[at(i), :width]),
            (wide_hi[...], wide_lo[...]), ((1,), (1,)),
        )
        part = part / (members - 1) + eye(i * rows)
        gram[at(i), :] = part
        return total + jnp.sum(part * part, keepdims=True)

    total = lax.fori_loop(0, chunks, gram_rows, jnp.zeros((1, 1), F32))
    frobenius = jnp.sqrt(total + 1e-06)

    def scale_rows(i, carry):
        gram[at(i), :] = gram[at(i), :] / frobenius
        return carry

    lax.fori_loop(0, chunks, scale_rows, 0)

    for repeat in range(NS_ITERS):
        last = repeat == NS_ITERS - 1

        def factor_rows(i, carry, repeat=repeat):
            now = gram[at(i), :]
            right_hi[at(i), :], right_lo[at(i), :] = split(1.5 * eye(i * rows) - 0.5 * now)
            left_hi[at(i), :], left_lo[at(i), :] = split(now)
            if repeat == 0:
                inv_hi[at(i), :], inv_lo[at(i), :] = right_hi[at(i), :], right_lo[at(i), :]
            return carry

        lax.fori_loop(0, chunks, factor_rows, 0)

        def step_rows(i, carry, repeat=repeat, last=last):
            right = (right_hi[...], right_lo[...])
            if not last:
                half = dot3((left_hi[at(i), :], left_lo[at(i), :]), right)
                gram[at(i), :] = dot3(split(half), right)
            if repeat > 0:
                inverse = dot3((inv_hi[at(i), :], inv_lo[at(i), :]), right)
                if last:
                    gram[at(i), :] = inverse / jnp.sqrt(frobenius)
                else:
                    inv_hi[at(i), :], inv_lo[at(i), :] = split(inverse)
            return carry

        lax.fori_loop(0, chunks, step_rows, 0)

    inner = jnp.sum(gram[...] * pull, axis=0, keepdims=True)
    shift = jnp.sum(gram[...] * inner, axis=1, keepdims=True) / (members - 1)

    def cut_rows(i, carry):
        inv_hi[at(i), :], inv_lo[at(i), :] = split(gram[at(i), :])
        return carry

    lax.fori_loop(0, chunks, cut_rows, 0)

    pltpu.make_async_copy(block.at[:others], block.at[:others], field_sem).wait()
    centre = jnp.mean(block[...], axis=0, keepdims=True)
    anomaly = block[...] - centre
    anom_hi[...], anom_lo[...] = split(anomaly)
    base = centre + jnp.sum(anomaly * shift, axis=0, keepdims=True)

    group = rows // per

    def back(k):
        return pltpu.make_async_remote_copy(
            result.at[pl.ds(pl.multiple_of(k * per, per), per), :], out_ref.at[mine],
            send_sem.at[4], back_sem, device_id=place(k), device_id_type=MESH,
        )

    def final_rows(i, carry):
        c = (me // group + i) % chunks
        result[at(c), :] = base + dot3(
            (inv_hi[at(c), :], inv_lo[at(c), :]), (anom_hi[...], anom_lo[...])
        )

        def send(j, inner_carry):
            k = c * group + (me + j) % group

            @pl.when(k != me)
            def _():
                back(k).start()

            return inner_carry

        return lax.fori_loop(0, group, send, carry)

    lax.fori_loop(0, chunks, final_rows, 0)
    out_ref[mine] = result[my_rows, :]

    pltpu.make_async_copy(out_ref.at[: count - 1], out_ref.at[: count - 1], back_sem).wait()
    pltpu.make_async_copy(seen.at[:others], seen.at[:others], send_sem.at[0]).wait()
    pltpu.make_async_copy(block.at[:others], block.at[:others], send_sem.at[1]).wait()
    pltpu.make_async_copy(block.at[:others], block.at[:others], send_sem.at[4]).wait()
    pltpu.make_async_copy(cells.at[: count - 1], cells.at[: count - 1], send_sem.at[5]).wait()


def whole(state, cx, cy, d, index, terms):
    per, count, lon = state.shape
    members, width = count * per, terms.shape[1]
    tall = count + 2 * FSTEPS
    square = (members, members)
    return pl.pallas_call(
        whole_kernel,
        out_shape=jax.ShapeDtypeStruct((count, per, lon), F32),
        in_specs=[pl.BlockSpec(memory_space=pl.ANY)] + [VMEM] * 5,
        out_specs=VMEM,
        scratch_shapes=[
            pltpu.VMEM(((FSTEPS + 1) * tall, per, lon), F32),
            pltpu.VMEM((5, count, lon), F32),
            pltpu.VMEM((tall, per, lon), F32),
            pltpu.VMEM((count, 1, width), jnp.int32),
            pltpu.VMEM((count, per, width), F32),
            pltpu.VMEM(terms.shape, F32),
            pltpu.VMEM((members, lon), F32),
            pltpu.VMEM((members, width), F32),
            pltpu.VMEM((3, members + 8, width), F32),
            pltpu.VMEM((members, lon), F32),
            pltpu.VMEM(square, F32),
        ]
        + [pltpu.VMEM(square, BF16)] * 6
        + [pltpu.VMEM((members, 3 * width), BF16)] * 2
        + [pltpu.VMEM((members, lon), BF16)] * 2
        + [
            pltpu.SemaphoreType.DMA,
            pltpu.SemaphoreType.DMA,
            pltpu.SemaphoreType.DMA((7,)),
            pltpu.SemaphoreType.DMA((2, 2)),
            pltpu.SemaphoreType.DMA((2, 2)),
        ]
        + [pltpu.SemaphoreType.DMA] * 7,
        compiler_params=pltpu.CompilerParams(
            collective_id=0, has_side_effects=True, vmem_limit_bytes=56 << 20
        ),
        cost_estimate=pl.CostEstimate(
            flops=10_000_000_000, bytes_accessed=6_000_000, transcendentals=0
        ),
    )(state, cx, cy, d, index, terms)


def on_device(starting_states, courant_x, courant_y, diffusion, obs_index, obs_value, loc_weight):
    terms = jnp.concatenate(
        [obs_value.reshape(1, -1), loc_weight.reshape(3, -1), jnp.zeros((4, obs_value.shape[2]), F32)]
    )
    out = whole(starting_states, courant_x, courant_y, diffusion, obs_index, terms)
    return jnp.transpose(out, (1, 0, 2))


def solution(mesh):
    in_specs = (
        P(("members", "blk"), "lat", None),
        P("lat", None),
        P("lat", None),
        P("lat", None),
        P("lat", ("members", "blk"), None),
        P("lat", ("members", "blk"), None),
        P("lat", ("members", "blk"), None, None),
    )
    out_specs = P(("members", "blk"), "lat", None)
    return jax.shard_map(
        on_device, mesh=mesh, in_specs=in_specs, out_specs=out_specs, check_vma=False
    )
```

profile of v0, /device:TPU:63, one launch (start us, length us, event | category | flops | bytes accessed | tf_op | source)
XLA Modules:
  0.0 135.1 jit_solution(9203716583086047172)
XLA Ops:
  0.0 0.1 pad.2.clone
  0.1 0.7 copy.11
  0.8 1.3 maximum_maximum_fusion.terms_ref
  2.1 130.0 %shard_map.73 = f32[64,8,768]{2,1,0:T(8,128)} custom-call(f32[8,64,768]{2,1,0:T(8,128)} %state_ref.1, f32[64,768]{1,0:T(8,128)} %cx_ref.1, f32[64,768]{1,0:T(8,128)} %cy_ref.1, f32[64,768]{1,0:T(8,128)} %d_ref.1, s32[1,1,128]{2,1,0:T(1,128)} %index_ref.1, f32[8,128]{1,0:T(8,128)} %maximum_maximum_fusion.terms_ref), custom_call_target="tpu_custom_call" | custom-call | flops 10000000000 | bytes 6000000 | tf_op jit(solution)/shard_map/pallas_call | solution.py:434
  132.1 3.1 %copy.8 = f32[8,64,768]{2,1,0:T(8,128)} copy(f32[8,64,768]{2,0,1:T(8,128)} %bitcast.5) | data formatting | bytes 3145728 | tf_op jit(solution)/shard_map/transpose | solution.py:477
  (1 shorter events, 0.0 us)
where the time goes:
time: 137 us; the launch traced here: 135 us
  Pallas kernels  130 us (95%)
  local copies, waits for them, and re-layouts  3.82 us (3%)
    pallas_call x1, Pallas kernels, whole(): pl.pallas_call(whole_kernel, out_shape=jax.ShapeDtypeStruct((count, per,...  130 us
    transpose x1, local copies, waits for them, and re-layouts, on_device(): return jnp.transpose(out, (1, 0, 2))  3.06 us

commit v1 on v0

v1 whole, which is shorter than its diff:
```python
import functools

import jax
import jax.numpy as jnp
from jax import lax
from jax.experimental import pallas as pl
from jax.experimental.pallas import tpu as pltpu
from jax.sharding import PartitionSpec as P

FSTEPS = 8
NS_ITERS = 4
ROWS = 16
EARLY = 2
AHEAD = 4
ALONE = 3
SPIRAL = (1, 7, 2, 6, 3, 5, 4, 0)
MESH = pl.DeviceIdType.MESH
VMEM = pl.BlockSpec(memory_space=pltpu.VMEM)
F32 = jnp.float32
BF16 = jnp.bfloat16


def split(x):
    high = x.astype(BF16)
    return high, (x - high.astype(F32)).astype(BF16)


def dot3(a, b, contract=((1,), (0,))):
    def one(p, q):
        return lax.dot_general(p, q, (contract, ((), ())), preferred_element_type=F32)

    return one(a[0], b[0]) + (one(a[0], b[1]) + one(a[1], b[0]))


def whole_kernel(
    state_ref, cx_ref, cy_ref, d_ref, index_ref, value_ref, weight_ref, out_ref,
    l0, l1, l2, l3, l4, l5, l6, l7, l8,
    dense, coef, cells, obs, value, weight, block, seen, stack, result,
    spread_ref, gram, left_hi, left_lo, right_hi, right_lo, inv_hi, inv_lo, wide_hi, wide_lo, field_hi, field_lo,
    load_sem, coef_sem, send_sem, edge_send, edge_recv,
    cell_sem, value_sem, weight_sem, obs_sem, field_sem, low_sem, high_sem, back_sem,
):
    levels = (l0, l1, l2, l3, l4, l5, l6, l7, l8)
    per, count, lon = state_ref.shape
    members = count * per
    tall = count + 2 * FSTEPS
    lo = lax.axis_index("members")
    bl = lax.axis_index("blk")
    lat = lax.axis_index("lat")
    n_lat = lax.axis_size("lat")
    n_blk = lax.axis_size("blk")
    me = lo * n_blk + bl
    my_z, my_y, my_core = (lo // 8) * 4 + bl, (lo // 2) % 4, lo % 2

    def set_at(z, y, core):
        return (((z // 4) * 4 + y) * 2 + core) * 4 + z % 4

    def block_at(z, y, core):
        return (z * 4 + y + (z % 2) * (3 - 2 * y)) * 2 + core

    def own_of(b):
        z, y = b // 8, (b // 2) % 4
        return set_at(z, y + (z % 2) * (3 - 2 * y), b % 2)

    def place(k):
        return {"members": k // n_blk, "blk": k % n_blk}

    zs = [lax.rem(my_z + dz, 8) for dz in range(8)]
    z_sets = [lax.div(z, 4) * 8 for z in zs]
    z_blks = [lax.rem(z, 4) for z in zs]

    def each(first, last, act):
        def group(q, carry):
            y = lax.rem(my_y + lax.div(q, 2), 4)
            core = lax.rem(my_core + lax.rem(q, 2), 2)
            even, odd = y * 2 + core, (3 - y) * 2 + core
            for dz in SPIRAL:
                z = zs[dz]
                m, blk = z_sets[dz] + even, z_blks[dz]
                b = z * 8 + even + lax.rem(z, 2) * (odd - even)
                run = functools.partial(act, {"members": m, "blk": blk}, m * 4 + blk, b, z)
                if dz == 0:
                    pl.when(q > 0)(run)
                else:
                    run()
            return carry

        lax.fori_loop(first, last, group, 0)

    mine = block_at(my_z, my_y, my_core)
    my_rows = pl.ds(pl.multiple_of(me * per, per), per)
    inner = pl.ds(FSTEPS, count)

    for m in range(per):
        pltpu.make_async_copy(state_ref.at[m], l0.at[inner, m, :], load_sem).start()

    barrier = pltpu.get_barrier_semaphore()

    @pl.when(lat > 0)
    def _():
        pl.semaphore_signal(barrier, inc=1, device_id={"lat": lat - 1}, device_id_type=MESH)

    @pl.when(lat < n_lat - 1)
    def _():
        pl.semaphore_signal(barrier, inc=1, device_id={"lat": lat + 1}, device_id_type=MESH)

    def greet(device, k, b, z):
        pl.semaphore_signal(barrier, inc=1, device_id=device, device_id_type=MESH)

    each(0, 8, greet)

    cx, cy, d = 0.5 * cx_ref[...], 0.5 * cy_ref[...], d_ref[...]
    for i, term in enumerate((1.0 - 4.0 * d, d - cx, d + cx, d - cy, d + cy)):
        dense[i] = term
        pltpu.make_async_copy(dense.at[i], coef.at[inner, i, :], coef_sem).start()
    cells[me] = index_ref[0]
    low_rows, high_rows = pl.ds(0, FSTEPS), pl.ds(FSTEPS + count, FSTEPS)

    @pl.when(lat == 0)
    def _():
        l0[low_rows] = jnp.zeros((FSTEPS, per, lon), F32)
        coef[low_rows] = jnp.zeros((FSTEPS, per, lon), F32)

    @pl.when(lat == n_lat - 1)
    def _():
        l0[high_rows] = jnp.zeros((FSTEPS, per, lon), F32)
        coef[high_rows] = jnp.zeros((FSTEPS, per, lon), F32)

    lane = lax.broadcasted_iota(jnp.int32, (per, 128), 1)
    parts = lon // 128

    def advance_row(step, r):
        old, new = levels[step - 1], levels[step]
        pieces = [old[r, :, p * 128 : (p + 1) * 128] for p in range(parts)]
        right = [pltpu.roll(v, 1, 1) for v in pieces]
        left = [pltpu.roll(v, 127, 1) for v in pieces]
        for p in range(parts):
            here = slice(p * 128, (p + 1) * 128)
            west = jnp.where(lane == 0, right[p - 1], right[p])
            east = jnp.where(lane == 127, left[(p + 1) % parts], left[p])
            c = [jnp.broadcast_to(coef[r, pl.ds(i, 1), here], lane.shape) for i in range(5)]
            new[r, :, here] = (
                (c[0] * pieces[p] + c[1] * east)
                + (c[2] * west + c[3] * old[r + 1, :, here])
                + c[4] * old[r - 1, :, here]
            )

    def inner_step(step):
        low, high = FSTEPS + step, FSTEPS + count - step

        def rows(i, carry):
            start = jnp.minimum(low + ROWS * i, high - ROWS)
            for u in range(ROWS):
                advance_row(step, start + u)
            return carry

        lax.fori_loop(0, (high - low + ROWS - 1) // ROWS, rows, 0)

    pltpu.make_async_copy(l0.at[inner], l0.at[inner], load_sem).wait()
    pltpu.make_async_copy(dense, dense, coef_sem).wait()
    for step in range(1, ALONE + 1):
        inner_step(step)
    pl.semaphore_wait(
        barrier, count - 1 + jnp.where(lat > 0, 1, 0) + jnp.where(lat < n_lat - 1, 1, 0)
    )

    def edges(up):
        source = pl.ds(count if up else FSTEPS, FSTEPS)
        target = low_rows if up else high_rows
        side = 0 if up else 1
        device = {"lat": lat + 1 if up else lat - 1}
        return [
            pltpu.make_async_remote_copy(
                l0.at[source], l0.at[target], edge_send.at[side, 0], edge_recv.at[side, 0],
                device_id=device, device_id_type=MESH,
            ),
            pltpu.make_async_remote_copy(
                coef.at[source], coef.at[target], edge_send.at[side, 1],
                edge_recv.at[side, 1], device_id=device, device_id_type=MESH,
            ),
        ]

    @pl.when(lat < n_lat - 1)
    def _():
        for copy in edges(True):
            copy.start()

    @pl.when(lat > 0)
    def _():
        for copy in edges(False):
            copy.start()

    def send_cells(device, k, b, z):
        pltpu.make_async_remote_copy(
            index_ref.at[0], cells.at[me], send_sem.at[5], cell_sem,
            device_id=device, device_id_type=MESH,
        ).start()

    each(0, 8, send_cells)

    def send_terms():
        owner = place(own_of(me))
        return [
            pltpu.make_async_remote_copy(
                value_ref.at[0], value, send_sem.at[6], value_sem,
                device_id=owner, device_id_type=MESH,
            ),
            pltpu.make_async_remote_copy(
                weight_ref.at[0, 0], weight, send_sem.at[7], weight_sem,
                device_id=owner, device_id_type=MESH,
            ),
        ]

    @pl.when(mine == me)
    def _():
        value[...] = value_ref[0]
        weight[...] = weight_ref[0, 0]

    @pl.when(mine != me)
    def _():
        for copy in send_terms():
            copy.start()

    for step in range(ALONE + 1, FSTEPS + 1):
        inner_step(step)

    def send_field(device, k, b, z):
        pltpu.make_async_remote_copy(
            l8.at[FSTEPS + b], block.at[my_rows, :], send_sem.at[1], field_sem,
            device_id=device, device_id_type=MESH,
        ).start()

    def away_from_edge(z):
        return (z > 0) & (z < 7)

    def send_early(device, k, b, z):
        pl.when(away_from_edge(z))(functools.partial(send_field, device, k, b, z))

    def send_late(device, k, b, z):
        pl.when(jnp.logical_not(away_from_edge(z)))(functools.partial(send_field, device, k, b, z))

    each(1, 1 + EARLY, send_early)

    @pl.when(lat > 0)
    def _():
        for copy in edges(True):
            copy.wait_recv()
        for copy in edges(False):
            copy.wait_send()

    @pl.when(lat < n_lat - 1)
    def _():
        for copy in edges(False):
            copy.wait_recv()
        for copy in edges(True):
            copy.wait_send()

    for step in range(1, FSTEPS + 1):
        for u in range(FSTEPS):
            advance_row(step, step + u)
            advance_row(step, tall - step - FSTEPS + u)

    pltpu.make_async_copy(cells.at[: count - 1], cells.at[: count - 1], cell_sem).wait()

    def observe(i, carry):
        for u in range(8):
            b = i * 8 + u
            index = jnp.broadcast_to(cells[b], lane.shape)
            where, group = jnp.bitwise_and(index, 127), jnp.right_shift(index, 7)
            found = jnp.zeros(lane.shape, F32)
            for p in range(parts):
                picked = jnp.take_along_axis(
                    l8[FSTEPS + b, :, p * 128 : (p + 1) * 128], where, axis=1
                )
                found = jnp.where(group == p, picked, found)
            obs[b] = found
        return carry

    lax.fori_loop(0, count // 8, observe, 0)

    def send_obs(device, k, b, z):
        pltpu.make_async_remote_copy(
            obs.at[b], seen.at[my_rows, :], send_sem.at[0], obs_sem,
            device_id=device, device_id_type=MESH,
        ).start()

    each(0, 8, send_obs)
    each(1, 1 + EARLY, send_late)
    each(1 + EARLY, 1 + AHEAD, send_field)
    seen[my_rows, :] = obs[mine]
    block[my_rows, :] = l8[FSTEPS + mine]

    @pl.when(mine != me)
    def _():
        for copy in send_terms():
            copy.wait()

    others = (count - 1) * per
    pltpu.make_async_copy(seen.at[:others], seen.at[:others], obs_sem).wait()

    ybar = jnp.mean(seen[...], axis=0, keepdims=True)
    own = seen[...] - ybar
    stack[1, :members, :] = own
    stack[1, members:, :] = jnp.broadcast_to(value[...] - ybar, (8, own.shape[1]))

    def to_low():
        return pltpu.make_async_remote_copy(
            stack.at[1], stack.at[2], send_sem.at[2], high_sem,
            device_id=place(own_of(mine - 1)), device_id_type=MESH,
        )

    def to_high():
        return pltpu.make_async_remote_copy(
            stack.at[1], stack.at[0], send_sem.at[3], low_sem,
            device_id=place(own_of(mine + 1)), device_id_type=MESH,
        )

    @pl.when(mine > 0)
    def _():
        to_low().start()

    @pl.when(mine < count - 1)
    def _():
        to_high().start()

    each(1 + AHEAD, 8, send_field)
    each(0, 1, send_field)

    @pl.when(mine == 0)
    def _():
        stack[0] = jnp.zeros(stack.shape[1:], F32)

    @pl.when(mine == count - 1)
    def _():
        stack[2] = jnp.zeros(stack.shape[1:], F32)

    @pl.when(mine > 0)
    def _():
        to_low().wait_send()
        to_high().wait_recv()

    @pl.when(mine < count - 1)
    def _():
        to_high().wait_send()
        to_low().wait_recv()

    obs = own.shape[1]
    pull_row = jnp.zeros((1, members), F32)
    for part in range(3):
        held = stack[part, :members, :]
        weighted = held * weight[pl.ds(part, 1), :]
        pull_row = pull_row + lax.dot_general(
            stack[part, pl.ds(members, 8), :], weighted, (((1,), (1,)), ((), ())),
            precision=lax.Precision.HIGHEST, preferred_element_type=F32,
        )[0:1]
        here = slice(part * obs, (part + 1) * obs)
        wide_hi[:, here], wide_lo[:, here] = split(held)
        left_hi[:, here], left_lo[:, here] = split(weighted)

    rows = 128
    chunks = members // rows

    def eye(start):
        row = lax.broadcasted_iota(jnp.int32, (rows, members), 0) + start
        return (row == lax.broadcasted_iota(jnp.int32, (rows, members), 1)).astype(F32)

    def at(i):
        return pl.ds(pl.multiple_of(i * rows, rows), rows)

    width = 3 * obs

    def gram_rows(i, total):
        part = dot3(
            (left_hi[at(i), :width], left_lo[at(i), :width]),
            (wide_hi[...], wide_lo[...]), ((1,), (1,)),
        )
        part = part / (members - 1) + eye(i * rows)
        gram[at(i), :] = part
        return total + jnp.sum(part * part, keepdims=True)

    total = lax.fori_loop(0, chunks, gram_rows, jnp.zeros((1, 1), F32))
    frobenius = jnp.sqrt(total + 1e-06)

    def scale_rows(i, carry):
        gram[at(i), :] = gram[at(i), :] / frobenius
        return carry

    lax.fori_loop(0, chunks, scale_rows, 0)

    for repeat in range(NS_ITERS):
        last = repeat == NS_ITERS - 1

        def factor_rows(i, carry, repeat=repeat):
            now = gram[at(i), :]
            right_hi[at(i), :], right_lo[at(i), :] = split(1.5 * eye(i * rows) - 0.5 * now)
            left_hi[at(i), :], left_lo[at(i), :] = split(now)
            if repeat == 0:
                inv_hi[at(i), :], inv_lo[at(i), :] = right_hi[at(i), :], right_lo[at(i), :]
            return carry

        lax.fori_loop(0, chunks, factor_rows, 0)

        def step_rows(i, carry, repeat=repeat, last=last):
            right = (right_hi[...], right_lo[...])
            if not last:
                half = dot3((left_hi[at(i), :], left_lo[at(i), :]), right)
                gram[at(i), :] = dot3(split(half), right)
            if repeat > 0:
                inverse = dot3((inv_hi[at(i), :], inv_lo[at(i), :]), right)
                if last:
                    gram[at(i), :] = inverse / jnp.sqrt(frobenius)
                else:
                    inv_hi[at(i), :], inv_lo[at(i), :] = split(inverse)
            return carry

        lax.fori_loop(0, chunks, step_rows, 0)

    inner = jnp.sum(gram[...] * pull_row, axis=1, keepdims=True)
    shift = jnp.sum(gram[...] * inner, axis=0, keepdims=True) / (members - 1)

    spread = 1.0 - jnp.sum(gram[...], axis=1, keepdims=True) - jnp.sum(shift, keepdims=True)
    spread_ref[...] = spread / members

    def cut_rows(i, carry):
        inv_hi[at(i), :], inv_lo[at(i), :] = split(
            gram[at(i), :] + shift + spread_ref[at(i), :]
        )
        return carry

    lax.fori_loop(0, chunks, cut_rows, 0)

    pltpu.make_async_copy(block.at[:others], block.at[:others], field_sem).wait()
    field_hi[...], field_lo[...] = split(block[...])

    group = rows // per
    low_bits = lax.rem(me, group)

    def back(k):
        return pltpu.make_async_remote_copy(
            result.at[pl.ds(pl.multiple_of(k * per, per), per), :], out_ref.at[mine],
            send_sem.at[4], back_sem, device_id=place(k), device_id_type=MESH,
        )

    def final_rows(i, carry):
        c = lax.rem(lax.div(me, group) + i, chunks)
        result[at(c), :] = dot3(
            (inv_hi[at(c), :], inv_lo[at(c), :]), (field_hi[...], field_lo[...])
        )

        for j in range(group):
            k = c * group + lax.rem(low_bits + j, group)

            @pl.when(k != me)
            def _(k=k):
                back(k).start()

        return carry

    lax.fori_loop(0, chunks, final_rows, 0)
    out_ref[mine] = result[my_rows, :]

    pltpu.make_async_copy(out_ref.at[: count - 1], out_ref.at[: count - 1], back_sem).wait()
    pltpu.make_async_copy(seen.at[:others], seen.at[:others], send_sem.at[0]).wait()
    pltpu.make_async_copy(block.at[:others], block.at[:others], send_sem.at[1]).wait()
    pltpu.make_async_copy(block.at[:others], block.at[:others], send_sem.at[4]).wait()
    pltpu.make_async_copy(cells.at[: count - 1], cells.at[: count - 1], send_sem.at[5]).wait()


def whole(state, cx, cy, d, index, value, weight):
    per, count, lon = state.shape
    members, width = count * per, value.shape[2]
    tall = count + 2 * FSTEPS
    square = (members, members)
    return pl.pallas_call(
        whole_kernel,
        out_shape=jax.ShapeDtypeStruct((count, per, lon), F32),
        in_specs=[pl.BlockSpec(memory_space=pl.ANY)] + [VMEM] * 6,
        out_specs=VMEM,
        scratch_shapes=[pltpu.VMEM((tall, per, lon), F32)] * (FSTEPS + 1)
        + [
            pltpu.VMEM((5, count, lon), F32),
            pltpu.VMEM((tall, per, lon), F32),
            pltpu.VMEM((count, 1, width), jnp.int32),
            pltpu.VMEM((count, per, width), F32),
            pltpu.VMEM((1, width), F32),
            pltpu.VMEM((3, width), F32),
            pltpu.VMEM((members, lon), F32),
            pltpu.VMEM((members, width), F32),
            pltpu.VMEM((3, members + 8, width), F32),
            pltpu.VMEM((members, lon), F32),
            pltpu.VMEM((members, 1), F32),
            pltpu.VMEM(square, F32),
        ]
        + [pltpu.VMEM(square, BF16)] * 6
        + [pltpu.VMEM((members, 3 * width), BF16)] * 2
        + [pltpu.VMEM((members, lon), BF16)] * 2
        + [
            pltpu.SemaphoreType.DMA,
            pltpu.SemaphoreType.DMA,
            pltpu.SemaphoreType.DMA((8,)),
            pltpu.SemaphoreType.DMA((2, 2)),
            pltpu.SemaphoreType.DMA((2, 2)),
        ]
        + [pltpu.SemaphoreType.DMA] * 8,
        compiler_params=pltpu.CompilerParams(
            collective_id=0, has_side_effects=True, vmem_limit_bytes=42 << 20
        ),
        cost_estimate=pl.CostEstimate(
            flops=10_000_000_000, bytes_accessed=6_000_000, transcendentals=0
        ),
    )(state, cx, cy, d, index, value, weight)


def on_device(starting_states, courant_x, courant_y, diffusion, obs_index, obs_value, loc_weight):
    out = whole(
        starting_states, courant_x, courant_y, diffusion, obs_index, obs_value, loc_weight
    )
    return jnp.transpose(out, (1, 0, 2))


def solution(mesh):
    in_specs = (
        P(("members", "blk"), "lat", None),
        P("lat", None),
        P("lat", None),
        P("lat", None),
        P("lat", ("members", "blk"), None),
        P("lat", ("members", "blk"), None),
        P("lat", ("members", "blk"), None, None),
    )
    out_specs = P(("members", "blk"), "lat", None)
    return jax.shard_map(
        on_device, mesh=mesh, in_specs=in_specs, out_specs=out_specs, check_vma=False
    )
```

time: 137 us -> 118 us (0.86); the launches traced: 135 us -> 118 us
  Pallas kernels: 130 us -> 110 us
  local copies, waits for them, and re-layouts: 3.82 us -> 7.8 us
    pallas_call x1, Pallas kernels: 130 us -> 110 us  [whole(): pl.pallas_call(whole_kernel, out_shape=jax.ShapeDtypeStruct((count, per,...]
    unnamed x1 -> x13, local copies, waits for them, and re-layouts: 0.68 us -> 6.18 us
    transpose x1, local copies, waits for them, and re-layouts: 3.06 us -> 1.62 us  [on_device(): return jnp.transpose(out, (1, 0, 2))]
where the time goes in v1:
time: 118 us
  Pallas kernels  110 us (93%)
  local copies, waits for them, and re-layouts  7.8 us (7%)
    pallas_call x1, Pallas kernels, whole(): pl.pallas_call(whole_kernel, out_shape=jax.ShapeDtypeStruct((count, per,...  110 us
    unnamed x13, local copies, waits for them, and re-layouts  6.18 us

profile of v1, /device:TPU:63, one launch (start us, length us, event | category | flops | bytes accessed | tf_op | source)
XLA Modules:
  0.0 118.1 jit_solution(10322523554559181654)
XLA Ops:
  0.0 0.7 copy.8.weight_ref
  0.7 0.0 copy-start
  0.7 1.4 %copy-done = f32[8,64,768]{2,1,0:T(8,128)S(1)} copy-done((f32[8,64,768]{2,1,0:T(8,128)S(1)}, f32[8,64,768]{2,1,0:T(8,128)}, u32[]{:S(2)}) %copy-start) | copy-done | bytes 1572888
  2.1 0.0 copy-start.1
  2.1 0.9 copy-done.1
  3.0 0.0 copy-start.2
  3.0 0.9 copy-done.2
  3.9 0.0 copy-start.3
  3.9 0.9 copy-done.3
  4.9 0.0 copy-start.4
  4.9 0.7 copy-done.4
  5.5 0.0 copy-start.5
  5.5 0.7 copy-done.5
  6.2 110.3 %shard_map.73 = f32[64,8,768]{2,1,0:T(8,128)S(1)} custom-call(f32[8,64,768]{2,1,0:T(8,128)S(1)} %copy-done, f32[64,768]{1,0:T(8,128)S(1)} %copy-done.1, f32[64,768]{1,0:T(8,128)S(1)} %copy-done.2, f32[64,768]{1,0:T(8,128)S(1)} %copy-done.3, s32[1,1,128]{2,1,0:T(1,128)S(1)} %copy-done.4, f32[1,1,128]{2,1,0:T(1,128)S(1)} %copy-done.5, ...), custom_call_target="tpu_custom_call" | custom-call | flops 10000000000 | bytes 6000000 | tf_op jit(solution)/shard_map/pallas_call | solution.py:474
  116.5 1.6 %copy.9 = f32[8,64,768]{2,1,0:T(8,128)} copy(f32[8,64,768]{2,0,1:T(8,128)S(1)} %bitcast.1) | data formatting | bytes 3145728 | tf_op jit(solution)/shard_map/transpose | solution.py:518
Async XLA Ops:
  0.7 1.4 %copy-start = (f32[8,64,768]{2,1,0:T(8,128)S(1)}, f32[8,64,768]{2,1,0:T(8,128)}, u32[]{:S(2)}) copy-start(f32[8,64,768]{2,1,0:T(8,128)} %state_ref.1) | copy-start | bytes 4718596
  2.1 0.9 copy-start.1
  3.0 0.9 copy-start.2
  3.9 0.9 copy-start.3
  4.9 0.7 copy-start.4
  5.5 0.7 copy-start.5

commit v2 on v1

--- a/solution.py
+++ b/solution.py
@@ -10,9 +10,9 @@
 FSTEPS = 8
 NS_ITERS = 4
 ROWS = 16
-EARLY = 2
-AHEAD = 4
-ALONE = 3
+EARLY = 0
+AHEAD = 2
+ALONE = 1
 SPIRAL = (1, 7, 2, 6, 3, 5, 4, 0)
 MESH = pl.DeviceIdType.MESH
 VMEM = pl.BlockSpec(memory_space=pltpu.VMEM)
@@ -35,9 +35,9 @@
 def whole_kernel(
     state_ref, cx_ref, cy_ref, d_ref, index_ref, value_ref, weight_ref, out_ref,
     l0, l1, l2, l3, l4, l5, l6, l7, l8,
-    dense, coef, cells, obs, value, weight, block, seen, stack, result,
+    raw, dense, coef, cells, obs, value, weight, block, seen, stack, result,
     spread_ref, gram, left_hi, left_lo, right_hi, right_lo, inv_hi, inv_lo, wide_hi, wide_lo, field_hi, field_lo,
-    load_sem, coef_sem, send_sem, edge_send, edge_recv,
+    load_sem, raw_sem, coef_sem, own_sem, send_sem, edge_send, edge_recv,
     cell_sem, value_sem, weight_sem, obs_sem, field_sem, low_sem, high_sem, back_sem,
 ):
     levels = (l0, l1, l2, l3, l4, l5, l6, l7, l8)
@@ -91,6 +91,9 @@
     my_rows = pl.ds(pl.multiple_of(me * per, per), per)
     inner = pl.ds(FSTEPS, count)
 
+    for i, ref in enumerate((cx_ref, cy_ref, d_ref)):
+        pltpu.make_async_copy(ref, raw.at[i], raw_sem).start()
+    pltpu.make_async_copy(index_ref.at[0], cells.at[me], own_sem.at[0]).start()
     for m in range(per):
         pltpu.make_async_copy(state_ref.at[m], l0.at[inner, m, :], load_sem).start()
 
@@ -109,11 +112,11 @@
 
     each(0, 8, greet)
 
-    cx, cy, d = 0.5 * cx_ref[...], 0.5 * cy_ref[...], d_ref[...]
+    pltpu.make_async_copy(raw, raw, raw_sem).wait()
+    cx, cy, d = 0.5 * raw[0], 0.5 * raw[1], raw[2]
     for i, term in enumerate((1.0 - 4.0 * d, d - cx, d + cx, d - cy, d + cy)):
         dense[i] = term
         pltpu.make_async_copy(dense.at[i], coef.at[inner, i, :], coef_sem).start()
-    cells[me] = index_ref[0]
     low_rows, high_rows = pl.ds(0, FSTEPS), pl.ds(FSTEPS + count, FSTEPS)
 
     @pl.when(lat == 0)
@@ -175,7 +178,7 @@
                 device_id=device, device_id_type=MESH,
             ),
             pltpu.make_async_remote_copy(
-                coef.at[source], coef.at[target], edge_send.at[side, 1],
+                coef.at[source, 0:5, :], coef.at[target, 0:5, :], edge_send.at[side, 1],
                 edge_recv.at[side, 1], device_id=device, device_id_type=MESH,
             ),
         ]
@@ -206,15 +209,21 @@
                 device_id=owner, device_id_type=MESH,
             ),
             pltpu.make_async_remote_copy(
-                weight_ref.at[0, 0], weight, send_sem.at[7], weight_sem,
+                weight_ref, weight, send_sem.at[7], weight_sem,
                 device_id=owner, device_id_type=MESH,
             ),
         ]
 
+    def keep_terms():
+        return [
+            pltpu.make_async_copy(value_ref.at[0], value, own_sem.at[1]),
+            pltpu.make_async_copy(weight_ref, weight, own_sem.at[2]),
+        ]
+
     @pl.when(mine == me)
     def _():
-        value[...] = value_ref[0]
-        weight[...] = weight_ref[0, 0]
+        for copy in keep_terms():
+            copy.start()
 
     @pl.when(mine != me)
     def _():
@@ -261,6 +270,7 @@
             advance_row(step, tall - step - FSTEPS + u)
 
     pltpu.make_async_copy(cells.at[: count - 1], cells.at[: count - 1], cell_sem).wait()
+    pltpu.make_async_copy(index_ref.at[0], cells.at[me], own_sem.at[0]).wait()
 
     def observe(i, carry):
         for u in range(8):
@@ -295,6 +305,11 @@
         for copy in send_terms():
             copy.wait()
 
+    @pl.when(mine == me)
+    def _():
+        for copy in keep_terms():
+            copy.wait()
+
     others = (count - 1) * per
     pltpu.make_async_copy(seen.at[:others], seen.at[:others], obs_sem).wait()
 
@@ -348,7 +363,7 @@
     pull_row = jnp.zeros((1, members), F32)
     for part in range(3):
         held = stack[part, :members, :]
-        weighted = held * weight[pl.ds(part, 1), :]
+        weighted = held * weight[part]
         pull_row = pull_row + lax.dot_general(
             stack[part, pl.ds(members, 8), :], weighted, (((1,), (1,)), ((), ())),
             precision=lax.Precision.HIGHEST, preferred_element_type=F32,
@@ -357,7 +372,7 @@
         wide_hi[:, here], wide_lo[:, here] = split(held)
         left_hi[:, here], left_lo[:, here] = split(weighted)
 
-    rows = 128
+    rows = 256
     chunks = members // rows
 
     def eye(start):
@@ -432,6 +447,8 @@
     pltpu.make_async_copy(block.at[:others], block.at[:others], field_sem).wait()
     field_hi[...], field_lo[...] = split(block[...])
 
+    rows = 128
+    chunks = members // rows
     group = rows // per
     low_bits = lax.rem(me, group)
 
@@ -471,19 +488,24 @@
     members, width = count * per, value.shape[2]
     tall = count + 2 * FSTEPS
     square = (members, members)
+    state, cx, cy, d, index, value, weight = [
+        pltpu.with_memory_space_constraint(x, pltpu.HBM)
+        for x in (state, cx, cy, d, index, value, weight)
+    ]
     return pl.pallas_call(
         whole_kernel,
         out_shape=jax.ShapeDtypeStruct((count, per, lon), F32),
-        in_specs=[pl.BlockSpec(memory_space=pl.ANY)] + [VMEM] * 6,
+        in_specs=[pl.BlockSpec(memory_space=pltpu.HBM)] * 7,
         out_specs=VMEM,
         scratch_shapes=[pltpu.VMEM((tall, per, lon), F32)] * (FSTEPS + 1)
         + [
+            pltpu.VMEM((3, count, lon), F32),
             pltpu.VMEM((5, count, lon), F32),
             pltpu.VMEM((tall, per, lon), F32),
             pltpu.VMEM((count, 1, width), jnp.int32),
             pltpu.VMEM((count, per, width), F32),
             pltpu.VMEM((1, width), F32),
-            pltpu.VMEM((3, width), F32),
+            pltpu.VMEM((3, 1, width), F32),
             pltpu.VMEM((members, lon), F32),
             pltpu.VMEM((members, width), F32),
             pltpu.VMEM((3, members + 8, width), F32),
@@ -497,6 +519,8 @@
         + [
             pltpu.SemaphoreType.DMA,
             pltpu.SemaphoreType.DMA,
+            pltpu.SemaphoreType.DMA,
+            pltpu.SemaphoreType.DMA((3,)),
             pltpu.SemaphoreType.DMA((8,)),
             pltpu.SemaphoreType.DMA((2, 2)),
             pltpu.SemaphoreType.DMA((2, 2)),
@@ -513,7 +537,8 @@
 
 def on_device(starting_states, courant_x, courant_y, diffusion, obs_index, obs_value, loc_weight):
     out = whole(
-        starting_states, courant_x, courant_y, diffusion, obs_index, obs_value, loc_weight
+        starting_states, courant_x, courant_y, diffusion, obs_index, obs_value,
+        loc_weight.reshape(3, 1, -1),
     )
     return jnp.transpose(out, (1, 0, 2))
 

time: 118 us -> 107 us (0.907)
  local copies, waits for them, and re-layouts: 7.8 us -> 1.62 us
  Pallas kernels: 110 us -> 105 us
    unnamed x13 -> x0, local copies, waits for them, and re-layouts: 6.18 us -> none
    pallas_call x1, Pallas kernels: 110 us -> 105 us  [whole(): pl.pallas_call(whole_kernel, out_shape=jax.ShapeDtypeStruct((count, per,...]
where the time goes in v2:
time: 107 us; the launch traced here: 106 us
  Pallas kernels  105 us (98%)
  local copies, waits for them, and re-layouts  1.62 us (2%)
    pallas_call x1, Pallas kernels, whole(): pl.pallas_call(whole_kernel, out_shape=jax.ShapeDtypeStruct((count, per,...  105 us

profile of v2, /device:TPU:63, one launch (start us, length us, event | category | flops | bytes accessed | tf_op | source)
XLA Modules:
  0.0 106.4 jit_solution(4110016470936293226)
XLA Ops:
  0.0 104.7 %shard_map.73 = f32[64,8,768]{2,1,0:T(8,128)S(1)} custom-call(f32[8,64,768]{2,1,0:T(8,128)} %state_ref.1, f32[64,768]{1,0:T(8,128)} %cx_ref.1, f32[64,768]{1,0:T(8,128)} %cy_ref.1, f32[64,768]{1,0:T(8,128)} %d_ref.1, s32[1,1,128]{2,1,0:T(1,128)} %index_ref.1, f32[1,1,128]{2,1,0:T(1,128)} %value_ref.1, f32[3,1,128]{2,1,0:T(1,128)} %bitcast.3), custom_call_target="tpu_custom_call" | custom-call | flops 10000000000 | bytes 6000000 | tf_op jit(solution)/shard_map/pallas_call | solution.py:495
  104.7 1.6 %copy.8 = f32[8,64,768]{2,1,0:T(8,128)} copy(f32[8,64,768]{2,0,1:T(8,128)S(1)} %bitcast.2) | data formatting | bytes 3145728 | tf_op jit(solution)/shard_map/transpose | solution.py:543

commit v3 on v2

--- a/solution.py
+++ b/solution.py
@@ -10,7 +10,7 @@
 FSTEPS = 8
 NS_ITERS = 4
 ROWS = 16
-EARLY = 0
+EARLY = 2
 AHEAD = 2
 ALONE = 1
 SPIRAL = (1, 7, 2, 6, 3, 5, 4, 0)
@@ -183,16 +183,6 @@
             ),
         ]
 
-    @pl.when(lat < n_lat - 1)
-    def _():
-        for copy in edges(True):
-            copy.start()
-
-    @pl.when(lat > 0)
-    def _():
-        for copy in edges(False):
-            copy.start()
-
     def send_cells(device, k, b, z):
         pltpu.make_async_remote_copy(
             index_ref.at[0], cells.at[me], send_sem.at[5], cell_sem,
@@ -200,6 +190,17 @@
         ).start()
 
     each(0, 8, send_cells)
+
+    @pl.when(lat < n_lat - 1)
+    def _():
+        for copy in edges(True):
+            copy.start()
+
+    @pl.when(lat > 0)
+    def _():
+        for copy in edges(False):
+            copy.start()
+
 
     def send_terms():
         owner = place(own_of(me))
@@ -247,27 +248,6 @@
 
     def send_late(device, k, b, z):
         pl.when(jnp.logical_not(away_from_edge(z)))(functools.partial(send_field, device, k, b, z))
-
-    each(1, 1 + EARLY, send_early)
-
-    @pl.when(lat > 0)
-    def _():
-        for copy in edges(True):
-            copy.wait_recv()
-        for copy in edges(False):
-            copy.wait_send()
-
-    @pl.when(lat < n_lat - 1)
-    def _():
-        for copy in edges(False):
-            copy.wait_recv()
-        for copy in edges(True):
-            copy.wait_send()
-
-    for step in range(1, FSTEPS + 1):
-        for u in range(FSTEPS):
-            advance_row(step, step + u)
-            advance_row(step, tall - step - FSTEPS + u)
 
     pltpu.make_async_copy(cells.at[: count - 1], cells.at[: count - 1], cell_sem).wait()
     pltpu.make_async_copy(index_ref.at[0], cells.at[me], own_sem.at[0]).wait()
@@ -286,7 +266,7 @@
             obs[b] = found
         return carry
 
-    lax.fori_loop(0, count // 8, observe, 0)
+    lax.fori_loop(1, count // 8 - 1, observe, 0)
 
     def send_obs(device, k, b, z):
         pltpu.make_async_remote_copy(
@@ -294,7 +274,38 @@
             device_id=device, device_id_type=MESH,
         ).start()
 
-    each(0, 8, send_obs)
+    def send_inner_obs(device, k, b, z):
+        pl.when(away_from_edge(z))(functools.partial(send_obs, device, k, b, z))
+
+    def send_edge_obs(device, k, b, z):
+        pl.when(jnp.logical_not(away_from_edge(z)))(functools.partial(send_obs, device, k, b, z))
+
+    each(0, 8, send_inner_obs)
+    each(1, 1 + EARLY, send_early)
+
+    @pl.when(lat > 0)
+    def _():
+        for copy in edges(True):
+            copy.wait_recv()
+        for copy in edges(False):
+            copy.wait_send()
+
+    @pl.when(lat < n_lat - 1)
+    def _():
+        for copy in edges(False):
+            copy.wait_recv()
+        for copy in edges(True):
+            copy.wait_send()
+
+    for step in range(1, FSTEPS + 1):
+        for u in range(FSTEPS):
+            advance_row(step, step + u)
+            advance_row(step, tall - step - FSTEPS + u)
+
+    lax.fori_loop(0, 1, observe, 0)
+    lax.fori_loop(count // 8 - 1, count // 8, observe, 0)
+
+    each(0, 8, send_edge_obs)
     each(1, 1 + EARLY, send_late)
     each(1 + EARLY, 1 + AHEAD, send_field)
     seen[my_rows, :] = obs[mine]

time: 107 us -> 104 us (0.972)
  Pallas kernels: 105 us -> 102 us
    pallas_call x1, Pallas kernels: 105 us -> 102 us  [whole(): pl.pallas_call(whole_kernel, out_shape=jax.ShapeDtypeStruct((count, per,...]
where the time goes in v3:
time: 104 us
  Pallas kernels  102 us (98%)
  local copies, waits for them, and re-layouts  1.62 us (2%)
    pallas_call x1, Pallas kernels, whole(): pl.pallas_call(whole_kernel, out_shape=jax.ShapeDtypeStruct((count, per,...  102 us

profile of v3, /device:TPU:63, one launch (start us, length us, event | category | flops | bytes accessed | tf_op | source)
XLA Modules:
  0.0 104.0 jit_solution(12818447742413390914)
XLA Ops:
  0.0 102.4 %shard_map.73 = f32[64,8,768]{2,1,0:T(8,128)S(1)} custom-call(f32[8,64,768]{2,1,0:T(8,128)} %state_ref.1, f32[64,768]{1,0:T(8,128)} %cx_ref.1, f32[64,768]{1,0:T(8,128)} %cy_ref.1, f32[64,768]{1,0:T(8,128)} %d_ref.1, s32[1,1,128]{2,1,0:T(1,128)} %index_ref.1, f32[1,1,128]{2,1,0:T(1,128)} %value_ref.1, f32[3,1,128]{2,1,0:T(1,128)} %bitcast.3), custom_call_target="tpu_custom_call" | custom-call | flops 10000000000 | bytes 6000000 | tf_op jit(solution)/shard_map/pallas_call | solution.py:506
  102.4 1.6 %copy.8 = f32[8,64,768]{2,1,0:T(8,128)} copy(f32[8,64,768]{2,0,1:T(8,128)S(1)} %bitcast.2) | data formatting | bytes 3145728 | tf_op jit(solution)/shard_map/transpose | solution.py:554

commit v4 on v3

--- a/solution.py
+++ b/solution.py
@@ -114,7 +114,7 @@
 
     pltpu.make_async_copy(raw, raw, raw_sem).wait()
     cx, cy, d = 0.5 * raw[0], 0.5 * raw[1], raw[2]
-    for i, term in enumerate((1.0 - 4.0 * d, d - cx, d + cx, d - cy, d + cy)):
+    for i, term in enumerate((d - cx, d + cx, d - cy, d + cy, 1.0 - 4.0 * d)):
         dense[i] = term
         pltpu.make_async_copy(dense.at[i], coef.at[inner, i, :], coef_sem).start()
     low_rows, high_rows = pl.ds(0, FSTEPS), pl.ds(FSTEPS + count, FSTEPS)
@@ -143,9 +143,9 @@
             east = jnp.where(lane == 127, left[(p + 1) % parts], left[p])
             c = [jnp.broadcast_to(coef[r, pl.ds(i, 1), here], lane.shape) for i in range(5)]
             new[r, :, here] = (
-                (c[0] * pieces[p] + c[1] * east)
-                + (c[2] * west + c[3] * old[r + 1, :, here])
-                + c[4] * old[r - 1, :, here]
+                (c[4] * pieces[p] + c[0] * east)
+                + (c[1] * west + c[2] * old[r + 1, :, here])
+                + c[3] * old[r - 1, :, here]
             )
 
     def inner_step(step):
@@ -178,7 +178,7 @@
                 device_id=device, device_id_type=MESH,
             ),
             pltpu.make_async_remote_copy(
-                coef.at[source, 0:5, :], coef.at[target, 0:5, :], edge_send.at[side, 1],
+                coef.at[source, 0:3, :], coef.at[target, 0:3, :], edge_send.at[side, 1],
                 edge_recv.at[side, 1], device_id=device, device_id_type=MESH,
             ),
         ]
@@ -296,6 +296,11 @@
             copy.wait_recv()
         for copy in edges(True):
             copy.wait_send()
+
+    for edge in (low_rows, high_rows):
+        twice = coef[edge, 0:1, :] + coef[edge, 1:2, :]
+        coef[edge, 3:4, :] = twice - coef[edge, 2:3, :]
+        coef[edge, 4:5, :] = 1.0 - 2.0 * twice
 
     for step in range(1, FSTEPS + 1):
         for u in range(FSTEPS):

time: 104 us -> 104 us (level)
  no operation moved by 1% of the time
where the time goes in v4:
time: 104 us
  Pallas kernels  102 us (98%)
  local copies, waits for them, and re-layouts  1.62 us (2%)
    pallas_call x1, Pallas kernels, whole(): pl.pallas_call(whole_kernel, out_shape=jax.ShapeDtypeStruct((count, per,...  102 us

profile of v4, /device:TPU:63, one launch (start us, length us, event | category | flops | bytes accessed | tf_op | source)
XLA Modules:
  0.0 104.0 jit_solution(15954973125127132465)
XLA Ops:
  0.0 102.4 %shard_map.73 = f32[64,8,768]{2,1,0:T(8,128)S(1)} custom-call(f32[8,64,768]{2,1,0:T(8,128)} %state_ref.1, f32[64,768]{1,0:T(8,128)} %cx_ref.1, f32[64,768]{1,0:T(8,128)} %cy_ref.1, f32[64,768]{1,0:T(8,128)} %d_ref.1, s32[1,1,128]{2,1,0:T(1,128)} %index_ref.1, f32[1,1,128]{2,1,0:T(1,128)} %value_ref.1, f32[3,1,128]{2,1,0:T(1,128)} %bitcast.3), custom_call_target="tpu_custom_call" | custom-call | flops 10000000000 | bytes 6000000 | tf_op jit(solution)/shard_map/pallas_call | solution.py:511
  102.4 1.6 %copy.8 = f32[8,64,768]{2,1,0:T(8,128)} copy(f32[8,64,768]{2,0,1:T(8,128)S(1)} %bitcast.2) | data formatting | bytes 3145728 | tf_op jit(solution)/shard_map/transpose | solution.py:559
